TPU v7x, 32 devices: a whole 2x2x4 slice. The times are simulated.
32 devices in a mesh: ctx: 16 (over z, y, x), exp: 2 (over core).
Axes of the slice: x: 2, y: 2, z: 4, core: 2. Of those that a mesh axis runs over, the one named last changes fastest.
Arguments:
- attn_query: bfloat16 [2048, 4096], P('ctx', 'exp'), may hold values from -3 to 3
- attn_key: bfloat16 [2048, 4096], P('ctx', 'exp'), may hold values from -3 to 3
- attn_value: bfloat16 [2048, 4096], P('ctx', 'exp'), may hold values from -6 to 6
- log_decay: float32 [32, 2048], P('exp', 'ctx'), may hold values from -1 to 0
- cotangent: bfloat16 [2048, 4096], P('ctx', 'exp'), may hold values from -6 to 6
- expert_input: bfloat16 [2048, 4096], P('ctx', 'exp'), may hold values from -6 to 6
- router_gates: bfloat16 [2048, 4], P('ctx'), may hold values from 0.049804688 to 0.59765625
- expert_ids: int32 [2048, 4], P('ctx'), may hold values from 0 to 15, all different within a row; in each aligned block of 128 rows (0 to 127, 128 to 255, ...) at most 40 rows name the same one
- up_weights: bfloat16 [16, 4096, 1536], P('ctx', 'exp'), may hold values from -0.09375 to 0.09375
- down_weights: bfloat16 [16, 1536, 4096], P('ctx', None, 'exp'), may hold values from -0.15625 to 0.15625
Outputs:
- query_grad: bfloat16 [2048, 4096], P('ctx', 'exp')
- key_grad: bfloat16 [2048, 4096], P('ctx', 'exp')
- value_grad: bfloat16 [2048, 4096], P('ctx', 'exp')
- input_grad: bfloat16 [2048, 4096], P('ctx', 'exp')
- gate_grad: bfloat16 [2048, 4], P('ctx')
Inputs may be any that keep to these rules, and one draw needn't show every extreme that they name: `expert_ids`: each row names 4 different experts. Within the rows of one device (each aligned block of 128 rows) no expert is named more than 40 times, a bound that some block reaches.
All inputs are finite; a program needn't handle non-finite values.
Results may differ from a plain program's by a relative error of at most 0.025.
Values may be sent and summed in bfloat16 or wider, within the bound.
No kernel may reach another device: no remote copies, remote signals or barrier semaphores. Data moves between devices by JAX's collectives and lax.ppermute only.
A program may use at most 128 MiB of HBM per device.

v0:
```python
import jax
import jax.numpy as jnp
from jax import lax
from jax.sharding import PartitionSpec as P


def prefix(value, axis, join, neutral, backward):
    count = lax.axis_size(axis)
    place = lax.axis_index(axis)
    ahead = count - 1 - place if backward else place
    gathered = jax.tree.map(
        lambda a, kind: lax.all_gather(a.astype(kind), axis), value, (jnp.bfloat16, jnp.bfloat16)
    )
    state = jax.tree.map(lambda a, e: jnp.zeros_like(a) + jnp.asarray(e, a.dtype), value, neutral)

    def one(step, state):
        source = count - 1 - step if backward else step
        return join(
            state,
            jax.tree.map(
                lambda a, own: lax.dynamic_index_in_dim(a, source, 0, False).astype(own.dtype),
                gathered,
                value,
            ),
        )

    return lax.fori_loop(0, ahead, one, state)


def silu_slope(pre_act):
    sigmoid_val = jax.nn.sigmoid(pre_act)
    return sigmoid_val * (1.0 + pre_act * (1.0 - sigmoid_val))


def chain_step(earlier, later):
    return (earlier[0] + later[0], jnp.exp(later[0])[:, None, None] * earlier[1] + later[1])


def attention_part(attn_query, attn_key, attn_value, log_decay, cotangent):
    length, features = attn_query.shape
    head_count = log_decay.shape[0]
    head_size = features // head_count
    head_shape = (length, head_count, head_size)
    query_heads = attn_query.reshape(head_shape)
    key_head_rows = attn_key.reshape(head_shape)
    value_head_rows = attn_value.reshape(head_shape)
    cotangent_heads = cotangent.reshape(head_shape)
    cumul = jnp.cumsum(log_decay, axis=1)
    block_gain = cumul[:, -1]
    head_gain = jnp.exp(cumul).T[:, :, None]
    tail_gain = jnp.exp(block_gain[:, None] - cumul).T[:, :, None]
    scaled_key_rows = (tail_gain * key_head_rows).astype(jnp.bfloat16)
    scaled_query_rows = (head_gain * query_heads).astype(jnp.bfloat16)
    local_state = jnp.einsum(
        "qcb,qce->cbe", scaled_key_rows, value_head_rows, preferred_element_type=jnp.float32
    )
    local_adjoint = jnp.einsum(
        "iuo,iuf->uof", scaled_query_rows, cotangent_heads, preferred_element_type=jnp.float32
    )
    identity = (
        jnp.zeros((head_count,), jnp.float32),
        jnp.zeros((head_count, head_size, head_size), jnp.float32),
    )
    state_in = prefix((block_gain, local_state), "ctx", chain_step, identity, False)
    adjoint_in = prefix((block_gain, local_adjoint), "ctx", chain_step, identity, True)
    state_bfloat_copy = state_in[1].astype(jnp.bfloat16)
    adjoint_bfloat_copy = adjoint_in[1].astype(jnp.bfloat16)
    row_index = lax.broadcasted_iota(jnp.int32, (length, length), 0)
    col_index = lax.broadcasted_iota(jnp.int32, (length, length), 1)
    causal = (row_index >= col_index)[None, :, :]
    spread = cumul[:, :, None] - cumul[:, None, :]
    decay_mask = jnp.where(causal, jnp.exp(jnp.where(causal, spread, 0.0)), 0.0)
    cross_terms = jnp.einsum(
        "thv,shv->hts", cotangent_heads, value_head_rows, preferred_element_type=jnp.float32
    )
    scores = jnp.einsum(
        "thk,shk->hts", query_heads, key_head_rows, preferred_element_type=jnp.float32
    )
    cross_weights = (cross_terms * decay_mask).astype(jnp.bfloat16)
    score_weights = (scores * decay_mask).astype(jnp.bfloat16)
    query_part = jnp.einsum(
        "hts,shk->thk", cross_weights, key_head_rows, preferred_element_type=jnp.float32
    )
    query_part = query_part + head_gain * jnp.einsum(
        "gmi,mli->gml", cotangent_heads, state_bfloat_copy, preferred_element_type=jnp.float32
    )
    key_part = jnp.einsum(
        "hts,thk->shk", cross_weights, query_heads, preferred_element_type=jnp.float32
    )
    key_part = key_part + tail_gain * jnp.einsum(
        "ecf,cpf->ecp", value_head_rows, adjoint_bfloat_copy, preferred_element_type=jnp.float32
    )
    value_part = jnp.einsum(
        "hts,thv->shv", score_weights, cotangent_heads, preferred_element_type=jnp.float32
    )
    value_part = value_part + tail_gain * jnp.einsum(
        "owr,wru->owu", key_head_rows, adjoint_bfloat_copy, preferred_element_type=jnp.float32
    )
    scale = 1.0 / head_size
    query_grad = (query_part * scale).reshape(length, features).astype(jnp.bfloat16)
    key_grad = (key_part * scale).reshape(length, features).astype(jnp.bfloat16)
    value_grad = (value_part * scale).reshape(length, features).astype(jnp.bfloat16)
    return (query_grad, key_grad, value_grad)


def expert_part(cotangent, expert_input, router_gates, expert_ids, up_weights, down_weights):
    tokens, feature_share = expert_input.shape
    top_count = expert_ids.shape[1]
    experts = lax.axis_size("ctx")
    capacity = 5 * tokens * top_count // (4 * experts)
    flat_ids = expert_ids.reshape(-1)
    onehot = (flat_ids[:, None] == jnp.arange(experts, dtype=jnp.int32)[None, :]).astype(jnp.int32)
    before = jnp.cumsum(onehot, axis=0) - onehot
    slot_index = jnp.sum(before * onehot, axis=1)
    target = (flat_ids * capacity + slot_index).reshape(tokens, top_count)
    placed = target[None, :, :] == jnp.arange(experts * capacity, dtype=jnp.int32)[:, None, None]
    placed_float = placed.astype(jnp.float32)
    dispatch_rows = jnp.sum(placed_float, axis=2).astype(jnp.bfloat16)
    buffer_in = jnp.dot(dispatch_rows, expert_input, preferred_element_type=jnp.float32).astype(
        jnp.bfloat16
    )
    buffer_cot = jnp.dot(dispatch_rows, cotangent, preferred_element_type=jnp.float32).astype(
        jnp.bfloat16
    )
    buffer_gate = jnp.einsum("jtk,tk->j", placed_float, router_gates.astype(jnp.float32)).astype(
        jnp.bfloat16
    )
    buffer_in = buffer_in.reshape(experts, capacity, feature_share)
    buffer_cot = buffer_cot.reshape(experts, capacity, feature_share)
    buffer_gate = buffer_gate.reshape(experts, capacity)
    up_local = up_weights[0]
    down_local = down_weights[0]
    inputs = lax.all_to_all(buffer_in, "ctx", split_axis=0, concat_axis=0, tiled=True)
    cot_rows = lax.all_to_all(buffer_cot, "ctx", split_axis=0, concat_axis=0, tiled=True)
    gate_rows = lax.all_to_all(buffer_gate, "ctx", split_axis=0, concat_axis=0, tiled=True)
    sources, item_count, share_width = inputs.shape
    flat_in = inputs.reshape(sources * item_count, share_width)
    flat_cot = cot_rows.reshape(sources * item_count, share_width)
    gate_col = gate_rows.reshape(-1).astype(jnp.float32)
    part_pre = jnp.dot(flat_in, up_local, preferred_element_type=jnp.float32)
    part_back = lax.dot_general(
        flat_cot, down_local, (((1,), (1,)), ((), ())), preferred_element_type=jnp.float32
    )
    pre_act = lax.psum(part_pre.astype(jnp.bfloat16), "exp").astype(jnp.float32)
    back_rows = lax.psum(part_back.astype(jnp.bfloat16), "exp").astype(jnp.float32)
    gate_back = jnp.sum(back_rows * jax.nn.silu(pre_act), axis=1)
    slope_rows = (gate_col[:, None] * back_rows * silu_slope(pre_act)).astype(jnp.bfloat16)
    rows_grad = lax.dot_general(
        slope_rows, up_local, (((1,), (1,)), ((), ())), preferred_element_type=jnp.float32
    )
    rows_grad = rows_grad.astype(jnp.bfloat16).reshape(sources, item_count, share_width)
    gate_back = gate_back.astype(jnp.bfloat16).reshape(sources, item_count)
    grad_buffer = lax.all_to_all(rows_grad, "ctx", split_axis=0, concat_axis=0, tiled=True)
    gate_buffer = lax.all_to_all(gate_back, "ctx", split_axis=0, concat_axis=0, tiled=True)
    grad_flat = grad_buffer.reshape(experts * capacity, feature_share)
    input_grad = lax.dot_general(
        dispatch_rows, grad_flat, (((0,), (0,)), ((), ())), preferred_element_type=jnp.float32
    )
    gate_grad = jnp.einsum("jtk,j->tk", placed_float, gate_buffer.reshape(-1).astype(jnp.float32))
    return (input_grad.astype(jnp.bfloat16), gate_grad.astype(jnp.bfloat16))


def body(
    attn_query,
    attn_key,
    attn_value,
    log_decay,
    cotangent,
    expert_input,
    router_gates,
    expert_ids,
    up_weights,
    down_weights,
):
    query_grad, key_grad, value_grad = attention_part(
        attn_query, attn_key, attn_value, log_decay, cotangent
    )
    input_grad, gate_grad = expert_part(
        cotangent, expert_input, router_gates, expert_ids, up_weights, down_weights
    )
    return (query_grad, key_grad, value_grad, input_grad, gate_grad)


def solution(mesh):
    return jax.shard_map(
        body,
        mesh=mesh,
        in_specs=(
            P("ctx", "exp"),
            P("ctx", "exp"),
            P("ctx", "exp"),
            P("exp", "ctx"),
            P("ctx", "exp"),
            P("ctx", "exp"),
            P("ctx", None),
            P("ctx", None),
            P("ctx", "exp", None),
            P("ctx", None, "exp"),
        ),
        out_specs=(
            P("ctx", "exp"),
            P("ctx", "exp"),
            P("ctx", "exp"),
            P("ctx", "exp"),
            P("ctx", None),
        ),
        check_vma=False,
    )
```

profile of v0, /device:TPU:31, one launch (start us, length us, event | category | flops | bytes accessed | tf_op | source)
XLA Modules:
  0.0 465.7 jit_solution(6112903337878251845)
XLA Ops:
  9.1 1.2 reduce-window.6
  11.6 3.4 convolution_convert_fusion.1
  15.0 6.4 %all-to-all-start.1 = ((bf16[16,40,2048]{2,1,0:T(8,128)(2,1)}), bf16[16,40,2048]{2,1,0:T(8,128)(2,1)S(1)}, u32[]{:S(2)}, u32[]{:S(2)}) async-start(bf16[16,40,2048]{2,1,0:T(8,128)(2,1)} %bitcast.22), calls=%async_computation.1 | async-start | bytes 5242880 | tf_op jit(solution)/shard_map/all_to_all | solution.py:134
  21.4 2.4 convolution_convert_fusion
  23.7 54.2 %all-to-all-done.1 = bf16[16,40,2048]{2,1,0:T(8,128)(2,1)S(1)} async-done(((bf16[16,40,2048]{2,1,0:T(8,128)(2,1)}), bf16[16,40,2048]{2,1,0:T(8,128)(2,1)S(1)}, u32[]{:S(2)}, u32[]{:S(2)}) %all-to-all-start.1) | async-done | bytes 2621472 | tf_op jit(solution)/shard_map/all_to_all | solution.py:134
  77.9 7.0 %all-to-all-start.2 = ((bf16[16,40,2048]{2,1,0:T(8,128)(2,1)}), bf16[16,40,2048]{2,1,0:T(8,128)(2,1)}, u32[]{:S(2)}, u32[]{:S(2)}) async-start(bf16[16,40,2048]{2,1,0:T(8,128)(2,1)} %bitcast.25), calls=%async_computation.2 | async-start | bytes 5242880 | tf_op jit(solution)/shard_map/all_to_all | solution.py:133
  85.0 8.3 %fusion.14 = bf16[640,1536]{1,0:T(8,128)(2,1)} fusion(bf16[640,2048]{1,0:T(8,128)(2,1)S(1)} %bitcast.160, bf16[1,1536,2048]{2,1,0:T(8,128)(2,1)} %param.23), kind=kOutput, calls=%fused_computation.23 | convolution fusion | flops 4027514880 | bytes 10878976 | tf_op jit(solution)/shard_map/dot_general | solution.py:141
  93.2 47.2 %all-to-all-done.2 = bf16[16,40,2048]{2,1,0:T(8,128)(2,1)} async-done(((bf16[16,40,2048]{2,1,0:T(8,128)(2,1)}), bf16[16,40,2048]{2,1,0:T(8,128)(2,1)}, u32[]{:S(2)}, u32[]{:S(2)}) %all-to-all-start.2) | async-done | bytes 2621472 | tf_op jit(solution)/shard_map/all_to_all | solution.py:133
  140.4 9.1 %fusion.17 = bf16[640,1536]{1,0:T(8,128)(2,1)} fusion(bf16[640,2048]{1,0:T(8,128)(2,1)} %bitcast.26, bf16[1,2048,1536]{2,1,0:T(8,128)(2,1)} %param.22), kind=kOutput, calls=%fused_computation.24 | convolution fusion | flops 4027514880 | bytes 10878976 | tf_op jit(solution)/shard_map/dot_general | solution.py:140
  149.7 0.9 copy-done.8
  151.7 1.3 convolution_convert_fusion.3
  153.4 1.1 convolution_convert_fusion.4
  155.0 9.3 %all_to_all.31 = bf16[16,1,40]{2,1,0:T(2,128)(2,1)S(1)} all-to-all(bf16[16,1,40]{2,1,0:T(2,128)(2,1)S(1)} %all_to_all.25), channel_id=1, replica_groups=mesh['ctx'=16,'exp'=2] {'ctx'}, dimensions={0} | all-to-all | bytes 2560 | tf_op jit(solution)/shard_map/all_to_all | solution.py:135
  164.4 14.2 %all-reduce.4.cloned.1.call-done = (bf16[640,1536]{1,0:T(8,128)(2,1)}, bf16[640,1536]{1,0:T(8,128)(2,1)}) async-done(((bf16[640,1536]{1,0:T(8,128)(2,1)}, bf16[640,1536]{1,0:T(8,128)(2,1)}), (bf16[640,1536]{1,0:T(8,128)(2,1)}, bf16[640,1536]{1,0:T(8,128)(2,1)})) %all-reduce.4.cloned.1.call-update) | async-done | bytes 3932176 | tf_op jit(solution)/shard_map/psum | solution.py:145
  178.6 3.4 fusion.8
  182.7 6.4 %all-to-all-start.4 = ((bf16[16,1,40]{2,1,0:T(2,128)(2,1)}), bf16[16,1,40]{2,1,0:T(2,128)(2,1)S(1)}, u32[]{:S(2)}, u32[]{:S(2)}) async-start(bf16[16,1,40]{2,1,0:T(2,128)(2,1)} %convert_element_type.212), calls=%async_computation.4 | async-start | bytes 16384 | tf_op jit(solution)/shard_map/all_to_all | solution.py:154
  189.1 10.5 %fusion.20 = bf16[640,2048]{1,0:T(8,128)(2,1)} fusion(bf16[1,2048,1536]{2,1,0:T(8,128)(2,1)} %param.22, bf16[640,1536]{1,0:T(8,128)(2,1)} %get-tuple-element.180, bf16[640,1536]{1,0:T(8,128)(2,1)} %get-tuple-element.181, f32[640]{0:T(1024)S(1)} %reshape.161), kind=kOutput, calls=%fused_computation.25 | convolution fusion | flops 4039639040 | bytes 12847616 | tf_op jit(solution)/shard_map/dot_general | solution.py:148
  199.6 6.4 %all-to-all-start.3 = ((bf16[16,40,2048]{2,1,0:T(8,128)(2,1)}), bf16[16,40,2048]{2,1,0:T(8,128)(2,1)S(1)}, u32[]{:S(2)}, u32[]{:S(2)}) async-start(bf16[16,40,2048]{2,1,0:T(8,128)(2,1)} %bitcast.159), calls=%async_computation.3 | async-start | bytes 5242880 | tf_op jit(solution)/shard_map/all_to_all | solution.py:153
  207.6 116.0 %all-reduce = bf16[256]{0:T(256)(128)(2,1)S(1)} all-reduce(bf16[256]{0:T(256)(128)(2,1)S(1)} %dynamic-update-slice), channel_id=2, replica_groups=mesh['ctx'=16,'exp'=2] {'ctx'}, use_global_device_ids=true, to_apply=%add | all-reduce | flops 256 | bytes 1024
  323.7 1.8 fusion.39
  326.3 1.5 convolution_bitcast_fusion.5
  328.7 1.4 convolution_convert_fusion.2
  330.3 1.0 copy-done.7
  331.3 1.6 fusion.31
  332.8 1.3 fusion.30
  334.2 93.8 %all-gather.6.cloned.1.call-done = bf16[256,128,128]{2,1,0:T(8,128)(2,1)} async-done(((bf16[16,128,128]{2,1,0:T(8,128)(2,1)}), bf16[256,128,128]{2,1,0:T(8,128)(2,1)}) %all-gather.6.cloned.1.call-update) | async-done | bytes 8388624 | tf_op jit(solution)/shard_map/all_gather | solution.py:12
  428.0 20.2 %while.26 = (s32[]{:T(128)}, f32[16,128,128]{2,1,0:T(8,128)S(1)}, s32[]{:T(128)}, bf16[16,16]{1,0:T(8,128)(2,1)S(1)}, bf16[16,16,128,128]{3,2,1,0:T(8,128)(2,1)}, /*index=5*/s32[]{:T(128)}, s32[]{:T(128)}, s32[]{:T(128)}) while((s32[]{:T(128)}, f32[16,128,128]{2,1,0:T(8,128)S(1)}, s32[]{:T(128)}, bf16[16,16]{1,0:T(8,128)(2,1)S(1)}, ...), condition=%wide.region_2.3_spmd, body=%wide.region_1.2_spmd.sunk | while | flops 786453 | bytes 2621735 | solution.py:27
  428.1 1.3 convert_add_fusion.4
  429.5 1.3 convert_add_fusion.4
  430.8 1.3 convert_add_fusion.4
  432.1 1.3 convert_add_fusion.4
  433.5 1.3 convert_add_fusion.4
  434.8 1.3 convert_add_fusion.4
  436.2 1.3 convert_add_fusion.4
  437.5 1.3 convert_add_fusion.4
  438.9 1.3 convert_add_fusion.4
  440.2 1.3 convert_add_fusion.4
  441.5 1.3 convert_add_fusion.4
  442.9 1.3 convert_add_fusion.4
  444.2 1.3 convert_add_fusion.4
  445.6 1.3 convert_add_fusion.4
  446.9 1.3 convert_add_fusion.4
  448.2 2.4 fusion.40
  450.6 2.1 copy.115
  452.7 1.5 fusion.37
  454.3 1.0 copy.116
  455.3 1.9 fusion.38
  457.2 1.0 copy.117
  (90 shorter events, 8.5 us)
Async XLA Ops:
  8.0 13.4 %copy-start = (bf16[128,2048]{1,0:T(8,128)(2,1)S(1)}, bf16[128,2048]{1,0:T(8,128)(2,1)}, u32[]{:S(2)}) copy-start(bf16[128,2048]{1,0:T(8,128)(2,1)} %param.19) | copy-start | bytes 1572868
  15.0 62.9 %all-to-all-start.1 = ((bf16[16,40,2048]{2,1,0:T(8,128)(2,1)}), bf16[16,40,2048]{2,1,0:T(8,128)(2,1)S(1)}, u32[]{:S(2)}, u32[]{:S(2)}) async-start(bf16[16,40,2048]{2,1,0:T(8,128)(2,1)} %bitcast.22), calls=%async_computation.1 | async-start | bytes 5242880 | tf_op jit(solution)/shard_map/all_to_all | solution.py:134
  77.9 62.5 %all-to-all-start.2 = ((bf16[16,40,2048]{2,1,0:T(8,128)(2,1)}), bf16[16,40,2048]{2,1,0:T(8,128)(2,1)}, u32[]{:S(2)}, u32[]{:S(2)}) async-start(bf16[16,40,2048]{2,1,0:T(8,128)(2,1)} %bitcast.25), calls=%async_computation.2 | async-start | bytes 5242880 | tf_op jit(solution)/shard_map/all_to_all | solution.py:133
  84.9 93.7 %all-reduce.4.cloned.1.call-start = ((), (), s32[]{:S(2)}) async-start(), calls=%async_computation.7 | async-start | bytes 7864320 | tf_op jit(solution)/shard_map/psum | solution.py:145
  149.5 1.0 copy-start.8
  149.5 1.3 copy-start.11
  149.5 1.6 copy-start.13
  149.6 3.5 copy-start.12
  149.6 3.8 copy-start.6
  149.6 4.9 %copy-start.14 = (bf16[128,4]{0,1:T(4,128)(2,1)S(1)}, bf16[128,4]{0,1:T(4,128)(2,1)}, u32[]{:S(2)}) copy-start(bf16[128,4]{0,1:T(4,128)(2,1)} %param.20) | copy-start | bytes 3076
  149.6 180.5 %all-gather.8.cloned.1.call-start = ((), (), s32[]{:S(2)}) async-start(), calls=%async_computation.6 | async-start | bytes 8912896 | tf_op jit(solution)/shard_map/all_gather | solution.py:12
  150.9 48.7 %copy-start.4 = (bf16[128,2048]{0,1:T(8,128)(2,1)}, bf16[128,2048]{0,1:T(8,128)(2,1)S(1)}, u32[]{:S(2)}) copy-start(bf16[128,2048]{0,1:T(8,128)(2,1)S(1)} %copy.124) | copy-start | bytes 1572868
  151.2 30.9 %copy-start.2 = (bf16[128,2048]{0,1:T(8,128)(2,1)}, bf16[128,2048]{0,1:T(8,128)(2,1)S(1)}, u32[]{:S(2)}) copy-start(bf16[128,2048]{0,1:T(8,128)(2,1)S(1)} %copy.101) | copy-start | bytes 1572868
  153.0 274.9 %all-gather.6.cloned.1.call-start = ((), (), s32[]{:S(2)}) async-start(), calls=%async_computation.5 | async-start | bytes 8912896 | tf_op jit(solution)/shard_map/all_gather | solution.py:12
  182.7 16.9 %all-to-all-start.4 = ((bf16[16,1,40]{2,1,0:T(2,128)(2,1)}), bf16[16,1,40]{2,1,0:T(2,128)(2,1)S(1)}, u32[]{:S(2)}, u32[]{:S(2)}) async-start(bf16[16,1,40]{2,1,0:T(2,128)(2,1)} %convert_element_type.212), calls=%async_computation.4 | async-start | bytes 16384 | tf_op jit(solution)/shard_map/all_to_all | solution.py:154
  199.6 6.4 %copy-start.15 = (u32[32]{0:T(128)S(1)}, u32[32]{0:T(128)}, u32[]{:S(2)}) copy-start(u32[32]{0:T(128)} %constant.80) | copy-start | bytes 388
  199.6 129.1 %all-to-all-start.3 = ((bf16[16,40,2048]{2,1,0:T(8,128)(2,1)}), bf16[16,40,2048]{2,1,0:T(8,128)(2,1)S(1)}, u32[]{:S(2)}, u32[]{:S(2)}) async-start(bf16[16,40,2048]{2,1,0:T(8,128)(2,1)} %bitcast.159), calls=%async_computation.3 | async-start | bytes 5242880 | tf_op jit(solution)/shard_map/all_to_all | solution.py:153
  325.5 0.8 copy-start.9
  330.2 1.0 copy-start.7
  428.0 20.2 %copy-start.5 = (bf16[128,2048]{0,1:T(8,128)(2,1)S(1)}, bf16[128,2048]{0,1:T(8,128)(2,1)}, u32[]{:S(2)}) copy-start(bf16[128,2048]{0,1:T(8,128)(2,1)} %copy-done.4) | copy-start | bytes 1572868
  448.2 4.5 copy-start.3
  448.2 4.5 copy-start.10
  450.6 7.6 %copy-start.1 = (bf16[128,2048]{1,0:T(8,128)(2,1)S(1)}, bf16[128,2048]{1,0:T(8,128)(2,1)}, u32[]{:S(2)}) copy-start(bf16[128,2048]{1,0:T(8,128)(2,1)} %param.19) | copy-start | bytes 1572868
Sparse Core Ops, SparseCore 0:
  149.7 28.8 all-reduce.3
Sparse Core Ops, SparseCore 1:
  153.4 160.4 all-gather.7
  317.1 110.8 all-gather.5
where the time goes:
time: 467 us; the launch traced here: 466 us
  waiting for transfers between devices  209 us (45%)
  blocking collectives  125 us (27%)
  matrix products  50 us (11%)
  other arithmetic  26.2 us (6%)
  starting transfers between devices  26.2 us (6%)
  between operations  16.4 us (4%)
  local copies, waits for them, and re-layouts  11.6 us (2%)
    unnamed x1, blocking collectives  116 us
    all_gather x2, waiting for transfers between devices, prefix(): lax.all_gather(a.astype(kind), axis)  93.8 us
    all_to_all x1, waiting for transfers between devices, expert_part(): lax.all_to_all(buffer_cot, 'ctx', split_axis=0, concat_axis=0, tiled=True)  54.2 us
    all_to_all x1, waiting for transfers between devices, expert_part(): lax.all_to_all(buffer_in, 'ctx', split_axis=0, concat_axis=0, tiled=True)  47.2 us
    add x15, other arithmetic, chain_step(): jnp.exp(later[0])[:, None, None] * earlier[1] + later[1]  19.5 us
    psum x1, waiting for transfers between devices, expert_part(): lax.psum(part_back.astype(jnp.bfloat16), 'exp').astype(jnp.float32)  14.2 us
    dot_general x1, matrix products, expert_part(): lax.dot_general(slope_rows, up_local, (((1,), (1,)), ((), ())), preferred...  10.5 us
  transfers between devices with their start and end apart: 7, of which 4 were waited for; matrix products, arithmetic and copies ran while one was open for 8% of the time, Pallas kernels for 0%

commit v1 on v0

--- a/solution.py
+++ b/solution.py
@@ -142,7 +142,9 @@
         flat_cot, down_local, (((1,), (1,)), ((), ())), preferred_element_type=jnp.float32
     )
     pre_act = lax.psum(part_pre.astype(jnp.bfloat16), "exp").astype(jnp.float32)
-    back_rows = lax.psum(part_back.astype(jnp.bfloat16), "exp").astype(jnp.float32)
+    back_rows = jnp.sum(lax.all_gather(part_back.astype(jnp.bfloat16), "exp"), axis=0).astype(
+        jnp.float32
+    )
     gate_back = jnp.sum(back_rows * jax.nn.silu(pre_act), axis=1)
     slope_rows = (gate_col[:, None] * back_rows * silu_slope(pre_act)).astype(jnp.bfloat16)
     rows_grad = lax.dot_general(

time: 467 us -> 482 us (1.032)
  waiting for transfers between devices: 209 us -> 237 us
  blocking collectives: 125 us -> 109 us
    all_gather x2, waiting for transfers between devices: 93.8 us -> 130 us  [prefix(): lax.all_gather(a.astype(kind), axis)]
    unnamed x1, blocking collectives: 116 us -> 100 us
    psum x1, waiting for transfers between devices: 14.2 us -> 6.06 us  [expert_part(): pre_act = lax.psum(part_pre.astype(jnp.bfloat16), 'exp').astype(jnp.float32)]
  transfers between devices with their start and end apart: 7 -> 8, of which waited for: 4 -> 5; matrix products, arithmetic and copies ran while one was open for 8% -> 11% of each run, Pallas kernels for 0% -> 0%
where the time goes in v1:
time: 482 us; the launch traced here: 480 us
  waiting for transfers between devices  237 us (49%)
  blocking collectives  109 us (23%)
  matrix products  49.5 us (10%)
  other arithmetic  29.7 us (6%)
  starting transfers between devices  26.3 us (5%)
  between operations  14.7 us (3%)
  local copies, waits for them, and re-layouts  13.5 us (3%)
    all_gather x2, waiting for transfers between devices, prefix(): lax.all_gather(a.astype(kind), axis)  130 us
    unnamed x1, blocking collectives  100 us
    all_to_all x1, waiting for transfers between devices, expert_part(): lax.all_to_all(buffer_cot, 'ctx', split_axis=0, concat_axis=0, tiled=True)  54.2 us
    all_to_all x1, waiting for transfers between devices, expert_part(): lax.all_to_all(buffer_in, 'ctx', split_axis=0, concat_axis=0, tiled=True)  46.1 us
    add x15, other arithmetic, chain_step(): jnp.exp(later[0])[:, None, None] * earlier[1] + later[1]  19.5 us
    unnamed x41, local copies, waits for them, and re-layouts  11 us
    dot_general x1, matrix products, expert_part(): lax.dot_general(slope_rows, up_local, (((1,), (1,)), ((), ())), preferred...  10 us
  transfers between devices with their start and end apart: 8, of which 5 were waited for; matrix products, arithmetic and copies ran while one was open for 11% of the time, Pallas kernels for 0%

profile of v1, /device:TPU:31, one launch (start us, length us, event | category | flops | bytes accessed | tf_op | source)
XLA Modules:
  0.0 480.3 jit_solution(3034554073323205026)
XLA Ops:
  8.3 1.2 reduce-window.6
  10.8 3.4 convolution_convert_fusion.1
  14.2 6.4 %all-to-all-start.1 = ((bf16[16,40,2048]{2,1,0:T(8,128)(2,1)}), bf16[16,40,2048]{2,1,0:T(8,128)(2,1)S(1)}, u32[]{:S(2)}, u32[]{:S(2)}) async-start(bf16[16,40,2048]{2,1,0:T(8,128)(2,1)} %bitcast.22), calls=%async_computation.1 | async-start | bytes 5242880 | tf_op jit(solution)/shard_map/all_to_all | solution.py:134
  20.6 2.3 convolution_convert_fusion
  22.9 54.2 %all-to-all-done.1 = bf16[16,40,2048]{2,1,0:T(8,128)(2,1)S(1)} async-done(((bf16[16,40,2048]{2,1,0:T(8,128)(2,1)}), bf16[16,40,2048]{2,1,0:T(8,128)(2,1)S(1)}, u32[]{:S(2)}, u32[]{:S(2)}) %all-to-all-start.1) | async-done | bytes 2621472 | tf_op jit(solution)/shard_map/all_to_all | solution.py:134
  77.2 1.5 copy-done.6
  78.7 7.0 %all-to-all-start.2 = ((bf16[16,40,2048]{2,1,0:T(8,128)(2,1)}), bf16[16,40,2048]{2,1,0:T(8,128)(2,1)S(1)}, u32[]{:S(2)}, u32[]{:S(2)}) async-start(bf16[16,40,2048]{2,1,0:T(8,128)(2,1)} %bitcast.26), calls=%async_computation.2 | async-start | bytes 5242880 | tf_op jit(solution)/shard_map/all_to_all | solution.py:133
  85.7 9.1 %fusion.14 = bf16[640,1536]{1,0:T(8,128)(2,1)} fusion(bf16[640,2048]{1,0:T(8,128)(2,1)} %bitcast.163, bf16[1,1536,2048]{2,1,0:T(8,128)(2,1)} %param.23), kind=kOutput, calls=%fused_computation.23 | convolution fusion | flops 4027514880 | bytes 10878976 | tf_op jit(solution)/shard_map/dot_general | solution.py:141
  94.9 46.1 %all-to-all-done.2 = bf16[16,40,2048]{2,1,0:T(8,128)(2,1)S(1)} async-done(((bf16[16,40,2048]{2,1,0:T(8,128)(2,1)}), bf16[16,40,2048]{2,1,0:T(8,128)(2,1)S(1)}, u32[]{:S(2)}, u32[]{:S(2)}) %all-to-all-start.2) | async-done | bytes 2621472 | tf_op jit(solution)/shard_map/all_to_all | solution.py:133
  141.1 8.3 %fusion.17 = bf16[640,1536]{1,0:T(8,128)(2,1)} fusion(bf16[640,2048]{1,0:T(8,128)(2,1)S(1)} %bitcast.162, bf16[1,2048,1536]{2,1,0:T(8,128)(2,1)} %param.22), kind=kOutput, calls=%fused_computation.24 | convolution fusion | flops 4027514880 | bytes 10878976 | tf_op jit(solution)/shard_map/dot_general | solution.py:140
  149.7 1.5 copy.101
  151.8 1.3 convolution_convert_fusion.3
  153.4 1.1 convolution_convert_fusion.4
  155.0 9.3 %all_to_all.31 = bf16[16,1,40]{2,1,0:T(2,128)(2,1)S(1)} all-to-all(bf16[16,1,40]{2,1,0:T(2,128)(2,1)S(1)} %all_to_all.25), channel_id=1, replica_groups=mesh['ctx'=16,'exp'=2] {'ctx'}, dimensions={0} | all-to-all | bytes 2560 | tf_op jit(solution)/shard_map/all_to_all | solution.py:135
  164.5 4.1 reduce_sum.44
  168.6 6.1 %all-reduce.3.cloned.1.call-done = bf16[640,1536]{1,0:T(8,128)(2,1)} async-done(((bf16[640,1536]{1,0:T(8,128)(2,1)}), bf16[640,1536]{1,0:T(8,128)(2,1)}) %all-reduce.3.cloned.1.call-update) | async-done | bytes 1966096 | tf_op jit(solution)/shard_map/psum | solution.py:144
  174.6 2.8 fusion.8
  178.1 6.4 %all-to-all-start.4 = ((bf16[16,1,40]{2,1,0:T(2,128)(2,1)}), bf16[16,1,40]{2,1,0:T(2,128)(2,1)S(1)}, u32[]{:S(2)}, u32[]{:S(2)}) async-start(bf16[16,1,40]{2,1,0:T(2,128)(2,1)} %convert_element_type.214), calls=%async_computation.4 | async-start | bytes 16384 | tf_op jit(solution)/shard_map/all_to_all | solution.py:156
  184.5 10.0 %fusion.20 = bf16[640,2048]{1,0:T(8,128)(2,1)} fusion(bf16[1,2048,1536]{2,1,0:T(8,128)(2,1)} %param.22, bf16[640,1536]{1,0:T(8,128)(2,1)S(1)} %reduce_sum.44, bf16[640,1536]{1,0:T(8,128)(2,1)} %all-reduce.3.cloned.1.call-done, f32[640]{0:T(1024)S(1)} %reshape.161), kind=kOutput, calls=%fused_computation.25 | convolution fusion | flops 4039639040 | bytes 12847616 | tf_op jit(solution)/shard_map/dot_general | solution.py:150
  194.5 6.5 %all-to-all-start.3 = ((bf16[16,40,2048]{2,1,0:T(8,128)(2,1)}), bf16[16,40,2048]{2,1,0:T(8,128)(2,1)S(1)}, u32[]{:S(2)}, u32[]{:S(2)}) async-start(bf16[16,40,2048]{2,1,0:T(8,128)(2,1)} %bitcast.161), calls=%async_computation.3 | async-start | bytes 5242880 | tf_op jit(solution)/shard_map/all_to_all | solution.py:155
  202.6 100.0 %all-reduce = bf16[256]{0:T(256)(128)(2,1)S(1)} all-reduce(bf16[256]{0:T(256)(128)(2,1)S(1)} %dynamic-update-slice), channel_id=2, replica_groups=mesh['ctx'=16,'exp'=2] {'ctx'}, use_global_device_ids=true, to_apply=%add | all-reduce | flops 256 | bytes 1024
  302.8 1.8 fusion.39
  305.4 1.5 convolution_bitcast_fusion.5
  307.8 1.4 convolution_convert_fusion.2
  309.2 19.1 %all-gather.10.cloned.1.call-done = bf16[256,128,128]{2,1,0:T(8,128)(2,1)} async-done(((bf16[16,128,128]{2,1,0:T(8,128)(2,1)}), bf16[256,128,128]{2,1,0:T(8,128)(2,1)}) %all-gather.10.cloned.1.call-update) | async-done | bytes 8388624 | tf_op jit(solution)/shard_map/all_gather | solution.py:12
  329.5 1.6 fusion.31
  331.0 1.3 fusion.30
  332.4 111.1 %all-gather.8.cloned.1.call-done = bf16[256,128,128]{2,1,0:T(8,128)(2,1)} async-done(((bf16[16,128,128]{2,1,0:T(8,128)(2,1)}), bf16[256,128,128]{2,1,0:T(8,128)(2,1)}) %all-gather.8.cloned.1.call-update) | async-done | bytes 8388624 | tf_op jit(solution)/shard_map/all_gather | solution.py:12
  443.6 20.2 %while.26 = (s32[]{:T(128)}, f32[16,128,128]{2,1,0:T(8,128)S(1)}, s32[]{:T(128)}, bf16[16,16]{1,0:T(8,128)(2,1)S(1)}, bf16[16,16,128,128]{3,2,1,0:T(8,128)(2,1)}, /*index=5*/s32[]{:T(128)}, s32[]{:T(128)}, s32[]{:T(128)}) while((s32[]{:T(128)}, f32[16,128,128]{2,1,0:T(8,128)S(1)}, s32[]{:T(128)}, bf16[16,16]{1,0:T(8,128)(2,1)S(1)}, ...), condition=%wide.region_2.3_spmd, body=%wide.region_1.2_spmd.sunk | while | flops 786453 | bytes 2621735 | solution.py:27
  443.6 1.3 convert_add_fusion.4
  445.0 1.3 convert_add_fusion.4
  446.3 1.3 convert_add_fusion.4
  447.7 1.3 convert_add_fusion.4
  449.0 1.3 convert_add_fusion.4
  450.4 1.3 convert_add_fusion.4
  451.7 1.3 convert_add_fusion.4
  453.1 1.3 convert_add_fusion.4
  454.4 1.3 convert_add_fusion.4
  455.7 1.3 convert_add_fusion.4
  457.1 1.3 convert_add_fusion.4
  458.4 1.3 convert_add_fusion.4
  459.8 1.3 convert_add_fusion.4
  461.1 1.3 convert_add_fusion.4
  462.4 1.3 convert_add_fusion.4
  463.8 2.4 fusion.40
  466.2 2.1 copy.115
  468.3 1.5 fusion.37
  470.8 1.9 fusion.38
  (94 shorter events, 11.3 us)
Async XLA Ops:
  7.2 13.4 %copy-start = (bf16[128,2048]{1,0:T(8,128)(2,1)S(1)}, bf16[128,2048]{1,0:T(8,128)(2,1)}, u32[]{:S(2)}) copy-start(bf16[128,2048]{1,0:T(8,128)(2,1)} %param.19) | copy-start | bytes 1572868
  14.2 62.9 %all-to-all-start.1 = ((bf16[16,40,2048]{2,1,0:T(8,128)(2,1)}), bf16[16,40,2048]{2,1,0:T(8,128)(2,1)S(1)}, u32[]{:S(2)}, u32[]{:S(2)}) async-start(bf16[16,40,2048]{2,1,0:T(8,128)(2,1)} %bitcast.22), calls=%async_computation.1 | async-start | bytes 5242880 | tf_op jit(solution)/shard_map/all_to_all | solution.py:134
  77.2 1.5 copy-start.6
  78.7 62.4 %all-to-all-start.2 = ((bf16[16,40,2048]{2,1,0:T(8,128)(2,1)}), bf16[16,40,2048]{2,1,0:T(8,128)(2,1)S(1)}, u32[]{:S(2)}, u32[]{:S(2)}) async-start(bf16[16,40,2048]{2,1,0:T(8,128)(2,1)} %bitcast.26), calls=%async_computation.2 | async-start | bytes 5242880 | tf_op jit(solution)/shard_map/all_to_all | solution.py:133
  85.7 78.8 %all-gather.12.cloned.1.call-start = ((), (), s32[]{:S(2)}) async-start(), calls=%async_computation.8 | async-start | bytes 5898240 | tf_op jit(solution)/shard_map/all_gather | solution.py:145
  94.9 79.8 %all-reduce.3.cloned.1.call-start = ((), (), s32[]{:S(2)}) async-start(), calls=%async_computation.5 | async-start | bytes 3932160 | tf_op jit(solution)/shard_map/psum | solution.py:144
  141.1 8.4 %copy-start.9 = (bf16[128,2048]{1,0:T(8,128)(2,1)S(1)}, bf16[128,2048]{1,0:T(8,128)(2,1)}, u32[]{:S(2)}) copy-start(bf16[128,2048]{1,0:T(8,128)(2,1)} %param.18) | copy-start | bytes 1572868
  149.3 1.9 copy-start.13
  149.3 3.8 copy-start.12
  149.3 4.1 copy-start.7
  149.4 5.2 %copy-start.14 = (bf16[128,4]{0,1:T(4,128)(2,1)S(1)}, bf16[128,4]{0,1:T(4,128)(2,1)}, u32[]{:S(2)}) copy-start(bf16[128,4]{0,1:T(4,128)(2,1)} %param.20) | copy-start | bytes 3076
  149.4 179.0 %all-gather.10.cloned.1.call-start = ((), (), s32[]{:S(2)}) async-start(), calls=%async_computation.7 | async-start | bytes 8912896 | tf_op jit(solution)/shard_map/all_gather | solution.py:12
  149.7 14.8 %copy-start.4 = (bf16[128,2048]{0,1:T(8,128)(2,1)}, bf16[128,2048]{0,1:T(8,128)(2,1)S(1)}, u32[]{:S(2)}) copy-start(bf16[128,2048]{0,1:T(8,128)(2,1)S(1)} %copy.124) | copy-start | bytes 1572868
  151.2 13.3 %copy-start.2 = (bf16[128,2048]{0,1:T(8,128)(2,1)}, bf16[128,2048]{0,1:T(8,128)(2,1)S(1)}, u32[]{:S(2)}) copy-start(bf16[128,2048]{0,1:T(8,128)(2,1)S(1)} %copy.101) | copy-start | bytes 1572868
  153.1 290.4 %all-gather.8.cloned.1.call-start = ((), (), s32[]{:S(2)}) async-start(), calls=%async_computation.6 | async-start | bytes 8912896 | tf_op jit(solution)/shard_map/all_gather | solution.py:12
  178.1 16.4 %all-to-all-start.4 = ((bf16[16,1,40]{2,1,0:T(2,128)(2,1)}), bf16[16,1,40]{2,1,0:T(2,128)(2,1)S(1)}, u32[]{:S(2)}, u32[]{:S(2)}) async-start(bf16[16,1,40]{2,1,0:T(2,128)(2,1)} %convert_element_type.214), calls=%async_computation.4 | async-start | bytes 16384 | tf_op jit(solution)/shard_map/all_to_all | solution.py:156
  194.5 6.5 %copy-start.15 = (u32[32]{0:T(128)S(1)}, u32[32]{0:T(128)}, u32[]{:S(2)}) copy-start(u32[32]{0:T(128)} %constant.82) | copy-start | bytes 388
  194.5 113.3 %all-to-all-start.3 = ((bf16[16,40,2048]{2,1,0:T(8,128)(2,1)}), bf16[16,40,2048]{2,1,0:T(8,128)(2,1)S(1)}, u32[]{:S(2)}, u32[]{:S(2)}) async-start(bf16[16,40,2048]{2,1,0:T(8,128)(2,1)} %bitcast.161), calls=%async_computation.3 | async-start | bytes 5242880 | tf_op jit(solution)/shard_map/all_to_all | solution.py:155
  304.6 0.8 copy-start.10
  328.4 1.0 copy-start.8
  443.6 20.2 %copy-start.5 = (bf16[128,2048]{0,1:T(8,128)(2,1)S(1)}, bf16[128,2048]{0,1:T(8,128)(2,1)}, u32[]{:S(2)}) copy-start(bf16[128,2048]{0,1:T(8,128)(2,1)} %copy-done.4) | copy-start | bytes 1572868
  463.7 4.5 copy-start.3
  463.8 4.5 copy-start.11
  466.2 7.6 %copy-start.1 = (bf16[128,2048]{1,0:T(8,128)(2,1)S(1)}, bf16[128,2048]{1,0:T(8,128)(2,1)}, u32[]{:S(2)}) copy-start(bf16[128,2048]{1,0:T(8,128)(2,1)} %param.19) | copy-start | bytes 1572868
Sparse Core Ops, SparseCore 0:
  95.0 16.2 all-gather.11
  149.5 25.1 all-reduce.2
  178.4 149.9 all-gather.9
  331.9 111.4 all-gather.7
